TPU v7x, 32 devices: a whole 2x2x4 slice. The times are simulated.
32 devices in a mesh: groups: 2 (over y), seq: 4 (over z), inner: 2 (over x), batch: 2 (over core).
Axes of the slice: x: 2, y: 2, z: 4, core: 2. Of those that a mesh axis runs over, the one named last changes fastest.
Arguments:
- queries: bfloat16 [4, 2048, 256], P(('groups', 'batch'), ('seq', 'inner')), parts along dimension 0, may hold values from -6 to 6
- keys: bfloat16 [4, 2048, 256], P(('groups', 'batch'), ('seq', 'inner')), parts along dimension 0, may hold values from -6 to 6
- values: bfloat16 [4, 2048, 256], P(('groups', 'batch'), ('seq', 'inner')), parts along dimension 0, may hold values from -6 to 6
- rates: float32 [4, 2048], P(('groups', 'batch'), ('seq', 'inner')), parts along dimension 0, may hold values from 0.05 to 1
- video_start: int32 [4], P(('groups', 'batch')), parts along dimension 0, may hold values from 0 to 511
- span_len: int32 [4, 4], P(('groups', 'batch'), 'seq'), parts along dimension 0, may hold values from 256 to 512, as said below
- init_weights: float32 [3, 256, 256], replicated, may hold values from -0.375 to 0.375
Outputs:
- outputs: bfloat16 [4, 2048, 256], P(('groups', 'batch'), ('seq', 'inner')), parts along dimension 0
- final_weights: float32 [4, 3, 256, 256], P(('groups', 'batch'), None, 'seq'), parts along dimension 0
There are 2 independent parts, one for each index of `groups`. A program takes and returns all parts, laid end to end along the dimension named above; an argument that names none is the same for every part. Nothing has to cross between parts.
Inputs may be any that keep to these rules, and one draw needn't show every extreme that they name: Every video has at least one span with span_len equal to 512.
All inputs are finite; a program needn't handle non-finite values.
Results may differ from a plain program's by a relative error of at most 0.015.
Values may be sent and summed in bfloat16 or wider, within the bound.
A program may use at most 64 MiB of HBM per device.

v0:
```python
import functools

import jax
import jax.numpy as jnp
from jax import lax
from jax.experimental import pallas as pl
from jax.experimental.pallas import tpu as pltpu
from jax.sharding import PartitionSpec as P

NS_STEPS = 5
CHUNKS = 4
MESH = pl.DeviceIdType.MESH
step_size = 0.1
norm_eps = 1e-07
column_eps = 1e-06
F32, BF16 = jnp.float32, jnp.bfloat16


def dot(a, b, ca, cb):
    return lax.dot_general(a, b, (((ca,), (cb,)), ((), ())), preferred_element_type=F32)


def apply_net(rows, w1, w3, w2):
    gate = dot(rows, w1, 1, 0)
    up = dot(rows, w3, 1, 0)
    hidden = (gate * jax.nn.sigmoid(gate) * up).astype(BF16)
    return dot(hidden, w2, 1, 1).astype(BF16)


def span_grads(k, nv, w1, w3, w2):
    gate = dot(k, w1, 1, 0)
    up = dot(k, w3, 1, 0)
    back = dot(nv, w2, 1, 0)
    s = jax.nn.sigmoid(gate)
    active = gate * s
    hidden = (active * up).astype(BF16)
    d_up = (back * active).astype(BF16)
    d_gate = (back * up * (s * (1.0 + gate * (1.0 - s)))).astype(BF16)
    return [dot(k, d_gate, 0, 0), dot(k, d_up, 0, 0), dot(nv, hidden, 0, 0)]


def newton(grads):
    xs = [g * (1.0 / (jnp.sqrt(jnp.sum(g * g, keepdims=True)) + norm_eps)) for g in grads]
    for unused in range(NS_STEPS):
        halves = [x.astype(BF16) for x in xs]
        grams = [dot(h, h, 1, 1).astype(BF16) for h in halves]
        xs = [1.5 * x - 0.5 * dot(g, h, 1, 0) for x, g, h in zip(xs, grams, halves)]
    return xs


def kernel(
    n, m, start_ref, len_ref, key_ref, value_ref, rate_ref, q_ref, init_ref, out_ref, final_ref,
    kv, queue, outs, state, norm, grad,
    give_send, give_recv, q_send, q_recv, o_send, o_recv, f_send, f_recv, z_recv, up_send, down_send,
):
    z, x = lax.axis_index("seq"), lax.axis_index("inner")
    chief = lax.rem(lax.axis_index("batch"), m)
    place = lax.rem(x - chief + m, m)
    active = place == 0
    tok = key_ref.shape[0]
    chunks, pair, part, head = kv.shape[2:]
    rows = final_ref.shape[1]
    mine = pl.ds(pl.multiple_of(z * rows, rows), rows)

    barrier = pltpu.get_barrier_semaphore()

    def greet(where):
        pl.semaphore_signal(barrier, inc=1, device_id=where, device_id_type=MESH)

    def helper(r):
        return {"inner": lax.rem(chief + r, m)}

    @pl.when(active)
    def _():
        pl.when(z > 0)(lambda: greet({"seq": z - 1}))
        pl.when(z < n - 1)(lambda: greet({"seq": z + 1}))
        for r in range(1, m):
            greet(helper(r))

    @pl.when(jnp.logical_not(active))
    def _():
        greet({"inner": chief})

    within = lax.broadcasted_iota(jnp.int32, (1, tok), 1) + x * tok
    position = within + z * (tok * m)
    valid = ((position >= start_ref[0]) & (within < len_ref[0, 0])).astype(F32)
    weight = rate_ref[...] * valid
    eye = lax.broadcasted_iota(jnp.int32, (tok, tok), 0) == lax.broadcasted_iota(
        jnp.int32, (tok, tok), 1
    )
    column = jnp.sum(jnp.where(eye, weight, 0.0), axis=1, keepdims=True)
    neg = (-(column * value_ref[...].astype(F32))).astype(BF16)
    for j in range(chunks):
        kv[z, place, j, 0] = key_ref[j * part : (j + 1) * part, :]
        kv[z, place, j, 1] = neg[j * part : (j + 1) * part, :]

    def copy(src, dst, send, recv, where):
        return pltpu.make_async_remote_copy(src, dst, send, recv, where, MESH)

    def give(r, j):
        block = kv.at[z, r, j]
        return copy(block, block, give_send.at[j], give_recv.at[r, j], {"inner": chief})

    def give_q(r):
        return copy(q_ref, queue.at[r], q_send.at[0], q_recv.at[r], {"inner": chief})

    def give_out(r):
        return copy(outs.at[r], out_ref, o_send.at[r], o_recv.at[0], helper(r))

    def give_final(r, i):
        return copy(state.at[i, mine], final_ref.at[i], f_send.at[r, i], f_recv.at[i], helper(r))

    def up(c, r, j):
        block = kv.at[c, r, j]
        return copy(block, block, up_send.at[c, r, j], z_recv.at[c, r, j], {"seq": z + 1})

    def down(c, r, j):
        block = kv.at[c, r, j]
        return copy(block, block, down_send.at[c, r, j], z_recv.at[c, r, j], {"seq": z - 1})

    @pl.when(jnp.logical_not(active))
    def _():
        pl.semaphore_wait(barrier, 1)
        for j in range(chunks):
            give(place, j).start()
        give_q(place).start()
        for j in range(chunks):
            give(place, j).wait_send()
        give_q(place).wait_send()
        give_out(0).wait_recv()
        for i in range(3):
            give_final(0, i).wait_recv()

    def relay_up(c, first, last):
        for r in range(first, last):
            for j in range(chunks):
                up(c, r, j).wait_recv()
                pl.when(z < n - 1)(lambda: up(c, r, j).start())

    def phase(p, first):
        pl.when(p < z)(lambda: relay_up(p, first, m))

        @pl.when((p == z - 1) & (z < n - 1))
        def _():
            for r in range(1, m):
                for j in range(chunks):
                    up(z, r, j).start()

        d = z + p

        @pl.when((d < n) & (d > z))
        def _():
            for r in range(m):
                for j in range(chunks):
                    down(d, r, j).wait_recv()
                    pl.when(z > 0)(lambda: down(d, r, j).start())

    @pl.when(active)
    def _():
        for i in range(3):
            w = init_ref[i]
            state[i] = w
            norm[i] = jnp.sum(w * w, axis=0, keepdims=True)
        pl.semaphore_wait(
            barrier, (m - 1) + (z > 0).astype(jnp.int32) + (z < n - 1).astype(jnp.int32)
        )
        for j in range(chunks):
            pl.when(z < n - 1)(lambda: up(z, 0, j).start())
            pl.when(z > 0)(lambda: down(z, 0, j).start())
        pl.when(z == 1)(lambda: relay_up(0, 0, 1))
        for r in range(1, m):
            for j in range(chunks):
                give(r, j).wait_recv()
                pl.when(z == 0)(lambda: up(z, r, j).start())
                pl.when(z > 0)(lambda: down(z, r, j).start())
        pl.when(z > 1)(lambda: relay_up(0, 0, 1))
        phase(0, 1)
        for r in range(1, m):
            give_q(r).wait_recv()

        @pl.loop(0, n)
        def _(c):
            w1, w3, w2 = [state[i].astype(BF16) for i in range(3)]

            @pl.when(c == z)
            def _():
                for r in range(1, m):
                    outs[r] = apply_net(queue[r], w1, w3, w2)
                out_ref[...] = apply_net(q_ref[...], w1, w3, w2)

            k = kv[c, :, :, 0].reshape(m * tok, head)
            nv = kv[c, :, :, 1].reshape(m * tok, head)
            for i, g in enumerate(span_grads(k, nv, w1, w3, w2)):
                grad[i] = g

            @pl.when(c == z)
            def _():
                for r in range(1, m):
                    give_out(r).start()

            xs = newton([grad[i] for i in range(3)])
            for i in range(3):
                moved = state[i] - step_size * xs[i].astype(BF16).astype(F32)
                after = jnp.sum(moved * moved, axis=0, keepdims=True)
                ratio = (norm[i] + column_eps) / (after + column_eps)
                state[i] = moved * jnp.sqrt(ratio)
                norm[i] = after * ratio
            phase(c + 1, 0)

        final_ref[...] = state[:, mine, :]
        for i in range(3):
            for r in range(1, m):
                give_final(r, i).start()

        @pl.loop(0, n)
        def _(c):
            for r in range(m):
                for j in range(chunks):
                    pl.when((c <= z) & (z < n - 1))(lambda: up(c, r, j).wait_send())
                    pl.when((c >= z) & (z > 0))(lambda: down(c, r, j).wait_send())

        for r in range(1, m):
            give_out(r).wait_send()
            for i in range(3):
                give_final(r, i).wait_send()


def per_device(queries, keys, values, rates, video_start, span_len, init_weights):
    tok, head = queries.shape[1:]
    n, m = lax.axis_size("seq"), lax.axis_size("inner")
    hidden = init_weights.shape[2]
    rows = init_weights.shape[1] // n
    vm = pl.BlockSpec(memory_space=pltpu.VMEM)
    sm = pl.BlockSpec(memory_space=pltpu.SMEM)
    dma = pltpu.SemaphoreType.DMA
    out, final = pl.pallas_call(
        functools.partial(kernel, n, m),
        out_shape=(
            jax.ShapeDtypeStruct((tok, head), BF16),
            jax.ShapeDtypeStruct((3, rows, hidden), F32),
        ),
        in_specs=[sm, sm, vm, vm, vm, vm, vm],
        out_specs=(vm, vm),
        scratch_shapes=[
            pltpu.VMEM((n, m, CHUNKS, 2, tok // CHUNKS, head), BF16),
            pltpu.VMEM((m, tok, head), BF16),
            pltpu.VMEM((m, tok, head), BF16),
            pltpu.VMEM(init_weights.shape, F32),
            pltpu.VMEM((3, 1, hidden), F32),
            pltpu.VMEM(init_weights.shape, F32),
            dma((CHUNKS,)),
            dma((m, CHUNKS)),
            dma((1,)),
            dma((m,)),
            dma((m,)),
            dma((1,)),
            dma((m, 3)),
            dma((3,)),
            dma((n, m, CHUNKS)),
            dma((n, m, CHUNKS)),
            dma((n, m, CHUNKS)),
        ],
        compiler_params=pltpu.CompilerParams(collective_id=0, has_side_effects=True),
    )(video_start, span_len, keys[0], values[0], rates, queries[0], init_weights)
    return out[None], final[None]


def solution(mesh):
    in_specs = (
        P(("groups", "batch"), ("seq", "inner"), None),
        P(("groups", "batch"), ("seq", "inner"), None),
        P(("groups", "batch"), ("seq", "inner"), None),
        P(("groups", "batch"), ("seq", "inner")),
        P(("groups", "batch")),
        P(("groups", "batch"), "seq"),
        P(),
    )
    out_specs = (
        P(("groups", "batch"), ("seq", "inner"), None),
        P(("groups", "batch"), None, "seq", None),
    )
    return jax.shard_map(
        per_device, mesh=mesh, in_specs=in_specs, out_specs=out_specs, check_vma=False
    )
```

profile of v0, /device:TPU:30, one launch (start us, length us, event | category | flops | bytes accessed | tf_op | source)
XLA Modules:
  0.0 43.9 jit_solution(13417254209868872361)
XLA Ops:
  1.9 39.7 %shard_map.86 = (bf16[256,256]{1,0:T(8,128)(2,1)}, f32[3,64,256]{2,1,0:T(8,128)}) custom-call(s32[1]{0:T(128)S(6)} %copy.11.start_ref, s32[1,1]{1,0:T(1,128)S(6)} %copy.12.len_ref, bf16[256,256]{1,0:T(8,128)(2,1)} %bitcast.6, bf16[256,256]{1,0:T(8,128)(2,1)} %bitcast.7, f32[1,256]{1,0:T(1,128)} %rate_ref.1, bf16[256,256]{1,0:T(8,128)(2,1)} %bitcast.8, ...), custom_call_target="tpu_custom_call" | custom-call | tf_op jit(solution)/shard_map/pallas_call | solution.py:236
  41.6 0.0 copy-start
  41.6 1.6 %copy.13 = bf16[1,256,256]{2,1,0:T(8,128)(2,1)} copy(bf16[1,256,256]{2,1,0:T(8,128)(2,1)} %bitcast.9) | data formatting | bytes 262144
  43.2 0.0 copy-done
  43.2 0.7 %copy.14 = f32[1,3,64,256]{3,2,1,0:T(8,128)} copy(f32[1,3,64,256]{3,2,1,0:T(8,128)S(1)} %bitcast.5) | data formatting | bytes 393216
Async XLA Ops:
  41.6 1.6 %copy-start = (f32[3,64,256]{2,1,0:T(8,128)S(1)}, f32[3,64,256]{2,1,0:T(8,128)}, u32[]{:S(2)}) copy-start(f32[3,64,256]{2,1,0:T(8,128)} %get-tuple-element.5) | copy-start | bytes 589828
where the time goes:
time: 44.1 us; the launch traced here: 43.9 us
  Pallas kernels  39.7 us (90%)
  local copies, waits for them, and re-layouts  2.29 us (5%)
  between operations  1.94 us (4%)
    pallas_call x1, Pallas kernels, per_device(): pl.pallas_call(functools.partial(kernel, n, m), out_shape=(jax.ShapeDtype...  39.7 us
    unnamed x4, local copies, waits for them, and re-layouts  2.29 us

commit v1 on v0

v1 whole, which is shorter than its diff:
```python
import functools

import jax
import jax.numpy as jnp
from jax import lax
from jax.experimental import pallas as pl
from jax.experimental.pallas import tpu as pltpu
from jax.sharding import PartitionSpec as P

NS_STEPS = 5
MESH = pl.DeviceIdType.MESH
step_size = 0.1
norm_eps = 1e-07
column_eps = 1e-06
half_root = 0.5**0.5
F32, BF16 = jnp.float32, jnp.bfloat16


def dot(a, b, ca, cb):
    return lax.dot_general(a, b, (((ca,), (cb,)), ((), ())), preferred_element_type=F32)


def sigmoid(g):
    return 0.5 + 0.5 * jnp.tanh(0.5 * g)


def apply_net(rows, w1, w3, w2):
    gate = dot(rows, w1, 1, 0)
    up = dot(rows, w3, 1, 0)
    hidden = (gate * sigmoid(gate) * up).astype(BF16)
    return dot(hidden, w2, 1, 1).astype(BF16)


def span_grads(k, nv, ws, scales):
    gate = dot(k, ws[0], 1, 0) * scales[0]
    up = dot(k, ws[1], 1, 0) * scales[1]
    back = dot(nv, ws[2], 1, 0) * scales[2]
    s = sigmoid(gate)
    active = gate * s
    hidden = (active * up).astype(BF16)
    d_up = (back * active).astype(BF16)
    d_gate = (back * up * (s + active - active * s)).astype(BF16)
    return [dot(k, d_gate, 0, 0), dot(k, d_up, 0, 0), dot(nv, hidden, 0, 0)]


def newton(grads):
    size = grads[0].shape[0]
    at = [lax.broadcasted_iota(jnp.int32, (size, size), d) for d in range(2)]
    eye = jnp.where(at[0] == at[1], 1.5, 0.0).astype(F32)
    xs = [g.astype(BF16) for g in grads]
    scales = [
        half_root / (jnp.sqrt(jnp.sum(g * g, keepdims=True)) + norm_eps) for g in grads
    ]
    factors = [(dot(x, x, 1, 1) * (s * s) - eye).astype(BF16) for x, s in zip(xs, scales)]
    ys = [dot(f, x, 1, 0) * s for f, x, s in zip(factors, xs, scales)]
    for unused in range(1, NS_STEPS):
        xs = [y.astype(BF16) for y in ys]
        factors = [(dot(x, x, 1, 1) - eye).astype(BF16) for x in xs]
        ys = [dot(f, x, 1, 0) for f, x in zip(factors, xs)]
    sign = -1.0 if NS_STEPS % 2 == 0 else 1.0
    return ys if sign > 0 else [-y for y in ys]


def kernel(
    n, m, nb, start_ref, len_ref, key_ref, value_ref, rate_ref, q_ref, init_ref, out_ref, final_ref,
    kv, queue, outs, halves, state, root, grad, fin, val_v, rate_v, q_v, nv_v,
    in_sem, kv_send, kv_recv, q_send, q_recv, h_send, h_recv, o_send, o_recv, f_send, f_recv,
    go, qgo,
):
    z, x, b = lax.axis_index("seq"), lax.axis_index("inner"), lax.axis_index("batch")
    tok, head = value_ref.shape
    rows = final_ref.shape[1]

    def master_of(v):
        return lax.rem(v, m), (n // 2) * (1 - lax.rem(v, 2))

    other = lax.rem(b + 1, nb)
    served = lax.rem(b + nb - 1, nb)
    mx, mz = master_of(b)
    sx, sz = master_of(served)
    is_master = (x == mx) & (z == mz)
    is_source = jnp.logical_not(is_master)
    is_server = (x == sx) & (z == sz)
    master = {"inner": mx, "seq": mz}
    server = {"inner": mx, "seq": mz, "batch": other}

    def same_side(lower):
        return (lower >= 0) & (lower + 1 < n) & ((lower + 1 < mz) | (lower > mz))

    has_next, has_prev = same_side(z), same_side(z - 1)
    upper = z > mz

    barrier = pltpu.get_barrier_semaphore()

    def greet(where):
        pl.semaphore_signal(barrier, inc=1, device_id=where, device_id_type=MESH)

    @pl.when(is_master)
    def _():
        @pl.loop(0, n)
        def _(c):
            for r in range(m):
                pl.when((c != mz) | (r != mx))(lambda: greet({"seq": c, "inner": r}))
        greet(server)

    @pl.when(is_server)
    def _():
        @pl.loop(0, n)
        def _(c):
            for r in range(m):
                greet({"seq": c, "inner": r, "batch": served})

    pl.when(has_prev)(lambda: greet({"seq": z - 1}))

    def fetch(src, dst, i):
        return pltpu.make_async_copy(src, dst, in_sem.at[i])

    get_val = fetch(value_ref, val_v, 0)
    get_rate = fetch(rate_ref, rate_v, 1)
    get_q = fetch(q_ref, q_v, 2)
    get_init = fetch(init_ref, state, 3)
    get_key = fetch(key_ref, kv.at[mz, mx, 0], 4)
    get_val.start()
    get_rate.start()
    pl.when(is_master)(get_key.start)
    pl.when(z == 0)(get_q.start)
    pl.when((z == 0) | is_master)(get_init.start)

    within = lax.broadcasted_iota(jnp.int32, (1, tok), 1) + x * tok
    position = within + z * (tok * m)
    valid = ((position >= start_ref[0]) & (within < len_ref[0, 0])).astype(F32)
    get_rate.wait()
    weight = rate_v[...] * valid
    eye = lax.broadcasted_iota(jnp.int32, (tok, tok), 0) == lax.broadcasted_iota(
        jnp.int32, (tok, tok), 1
    )
    column = jnp.sum(jnp.where(eye, weight, 0.0), axis=1, keepdims=True)
    get_val.wait()
    neg = (-(column * val_v[...].astype(F32))).astype(BF16)
    nv_v[...] = neg

    pl.semaphore_wait(
        barrier,
        1 + is_source.astype(jnp.int32) + is_server.astype(jnp.int32) + has_next.astype(jnp.int32),
    )

    def copy(src, dst, send, recv, where):
        return pltpu.make_async_remote_copy(src, dst, send, recv, where, MESH)

    give_k = copy(key_ref, kv.at[z, x, 0], kv_send.at[0], kv_recv.at[z, x, 0], master)
    give_nv = copy(nv_v, kv.at[z, x, 1], kv_send.at[1], kv_recv.at[z, x, 1], master)
    give_q = copy(q_ref, queue.at[z, x], q_send, q_recv.at[z, x], server)

    def take(c, r, j):
        return copy(kv.at[c, r, j], kv.at[c, r, j], kv_send.at[j], kv_recv.at[c, r, j], master)

    def give_half(c):
        return copy(halves.at[c], halves.at[c], h_send.at[c], h_recv.at[c], server)

    def give_out(c, r):
        where = {"seq": c, "inner": r, "batch": served}
        return copy(outs.at[c, r], out_ref, o_send.at[c, r], o_recv, where)

    def give_final(c, r, i):
        mine = pl.ds(pl.multiple_of(c * rows, rows), rows)
        where = {"seq": c, "inner": r}
        return copy(fin.at[i, mine], final_ref.at[i], f_send.at[c, r, i], f_recv.at[i], where)

    @pl.when(is_source)
    def _():
        pl.when(has_prev)(lambda: pl.semaphore_wait(go, 1))
        give_k.start()
        give_nv.start()

        @pl.when(has_next)
        def _():
            pl.semaphore_signal(go, inc=1, device_id={"seq": z + 1}, device_id_type=MESH)
            pl.when(upper)(lambda: pl.semaphore_wait(qgo, 1))

    @pl.when(z > 0)
    def _():
        give_q.start()

        @pl.when(has_prev & upper)
        def _():
            pl.semaphore_signal(qgo, inc=1, device_id={"seq": z - 1}, device_id_type=MESH)

    pl.when((z == 0) | is_master)(get_init.wait)

    @pl.when(z == 0)
    def _():
        get_q.wait()
        out_ref[...] = apply_net(q_v[...], *[state[i].astype(BF16) for i in range(3)])

    def sums(i):
        w = state[i]
        after = jnp.sum(w * w, axis=0, keepdims=True)
        scale = root[i] * lax.rsqrt(after + column_eps)
        total = after * (scale * scale) + column_eps
        root[i] = total * lax.rsqrt(total)
        return scale

    @pl.when(is_master)
    def _():
        for i in range(3):
            w = state[i]
            root[i] = jnp.sqrt(jnp.sum(w * w, axis=0, keepdims=True) + column_eps)
        kv[mz, mx, 1] = nv_v[...]
        get_key.wait()

        @pl.loop(0, n)
        def _(c):
            for r in range(m):
                for j in range(2):
                    pl.when((c != mz) | (r != mx))(lambda: take(c, r, j).wait_recv())
            scales = [sums(i) for i in range(3)]
            ws = [state[i].astype(BF16) for i in range(3)]
            k = kv[c, :, 0].reshape(m * tok, head)
            nv = kv[c, :, 1].reshape(m * tok, head)
            for i, g in enumerate(span_grads(k, nv, ws, scales)):
                grad[i] = g
            for i in range(3):
                w = state[i] * scales[i]
                state[i] = w
                halves[c, i] = w.astype(BF16)
            ys = newton([grad[i] for i in range(3)])
            pl.when(c > 0)(lambda: give_half(c).start())
            for i in range(3):
                state[i] = state[i] + (step_size / half_root) * ys[i]

        for i in range(3):
            fin[i] = (state[i] * sums(i)).astype(BF16)

        @pl.loop(0, n)
        def _(d):
            c = n - 1 - d
            for r in range(m):
                for i in range(3):
                    pl.when((c != mz) | (r != mx))(lambda: give_final(c, r, i).start())

        mine = pl.ds(pl.multiple_of(z * rows, rows), rows)
        final_ref[...] = fin[:, mine, :]

        @pl.loop(0, n)
        def _(c):
            for r in range(m):
                for i in range(3):
                    pl.when((c != mz) | (r != mx))(lambda: give_final(c, r, i).wait_send())
            pl.when(c > 0)(lambda: give_half(c).wait_send())

    @pl.when(is_server)
    def _():
        @pl.loop(1, n)
        def _(c):
            for r in range(m):
                copy(queue.at[c, r], queue.at[c, r], q_send, q_recv.at[c, r], server).wait_recv()
            give_half(c).wait_recv()
            ws = [halves[c, i] for i in range(3)]
            for r in range(m):
                outs[c, r] = apply_net(queue[c, r], *ws)
                give_out(c, r).start()

        @pl.loop(1, n)
        def _(c):
            for r in range(m):
                give_out(c, r).wait_send()

    @pl.when(is_source)
    def _():
        give_k.wait_send()
        give_nv.wait_send()
        for i in range(3):
            give_final(0, 0, i).wait_recv()

    @pl.when(z > 0)
    def _():
        give_q.wait_send()
        give_out(0, 0).wait_recv()


def finish(out_ref, final_ref, out_hbm, final_hbm, wide, sem):
    first = pltpu.make_async_copy(out_ref, out_hbm, sem.at[0])
    first.start()
    wide[...] = final_ref[...].astype(F32)
    second = pltpu.make_async_copy(wide, final_hbm, sem.at[1])
    second.start()
    first.wait()
    second.wait()


def per_device(queries, keys, values, rates, video_start, span_len, init_weights):
    tok, head = queries.shape[1:]
    n, m, nb = lax.axis_size("seq"), lax.axis_size("inner"), lax.axis_size("batch")
    hidden = init_weights.shape[2]
    rows = init_weights.shape[1] // n
    vm = pl.BlockSpec(memory_space=pltpu.VMEM)
    sm = pl.BlockSpec(memory_space=pltpu.SMEM)
    hbm = pl.BlockSpec(memory_space=pl.ANY)
    dma = pltpu.SemaphoreType.DMA
    out, final = pl.pallas_call(
        functools.partial(kernel, n, m, nb),
        out_shape=(
            jax.ShapeDtypeStruct((tok, head), BF16),
            jax.ShapeDtypeStruct((3, rows, hidden), BF16),
        ),
        in_specs=[sm, sm, hbm, hbm, hbm, hbm, hbm],
        out_specs=(vm, vm),
        scratch_shapes=[
            pltpu.VMEM((n, m, 2, tok, head), BF16),
            pltpu.VMEM((n, m, tok, head), BF16),
            pltpu.VMEM((n, m, tok, head), BF16),
            pltpu.VMEM((n,) + init_weights.shape, BF16),
            pltpu.VMEM(init_weights.shape, F32),
            pltpu.VMEM((3, 1, hidden), F32),
            pltpu.VMEM(init_weights.shape, F32),
            pltpu.VMEM(init_weights.shape, BF16),
            pltpu.VMEM((tok, head), BF16),
            pltpu.VMEM((1, tok), F32),
            pltpu.VMEM((tok, head), BF16),
            pltpu.VMEM((tok, head), BF16),
            dma((5,)),
            dma((2,)),
            dma((n, m, 2)),
            dma(()),
            dma((n, m)),
            dma((n,)),
            dma((n,)),
            dma((n, m)),
            dma(()),
            dma((n, m, 3)),
            dma((3,)),
            pltpu.SemaphoreType.REGULAR,
            pltpu.SemaphoreType.REGULAR,
        ],
        compiler_params=pltpu.CompilerParams(collective_id=0, has_side_effects=True),
    )(video_start, span_len, keys[0], values[0], rates, queries[0], init_weights)
    out, final = pl.pallas_call(
        finish,
        out_shape=(
            jax.ShapeDtypeStruct((tok, head), BF16),
            jax.ShapeDtypeStruct((3, rows, hidden), F32),
        ),
        in_specs=[vm, vm],
        out_specs=(hbm, hbm),
        scratch_shapes=[pltpu.VMEM((3, rows, hidden), F32), dma((2,))],
    )(out, final)
    return out[None], final[None]


def solution(mesh):
    in_specs = (
        P(("groups", "batch"), ("seq", "inner"), None),
        P(("groups", "batch"), ("seq", "inner"), None),
        P(("groups", "batch"), ("seq", "inner"), None),
        P(("groups", "batch"), ("seq", "inner")),
        P(("groups", "batch")),
        P(("groups", "batch"), "seq"),
        P(),
    )
    out_specs = (
        P(("groups", "batch"), ("seq", "inner"), None),
        P(("groups", "batch"), None, "seq", None),
    )
    return jax.shard_map(
        per_device, mesh=mesh, in_specs=in_specs, out_specs=out_specs, check_vma=False
    )
```

time: 44.1 us -> 46.7 us (1.059)
  the two profiles are of different devices: /device:TPU:30 before, /device:TPU:15 now
where the time goes in v1:
time: 46.7 us; the launch traced here: 46.5 us
  Pallas kernels  44.6 us (96%)
  between operations  1.93 us (4%)
    pallas_call x1, Pallas kernels, per_device(): pl.pallas_call(functools.partial(kernel, n, m, nb), out_shape=(jax.ShapeD...  42.9 us
    pallas_call x1, Pallas kernels, per_device(): pl.pallas_call(finish, out_shape=(jax.ShapeDtypeStruct((tok, head), BF16)...  1.69 us

profile of v1, /device:TPU:15, one launch (start us, length us, event | category | flops | bytes accessed | tf_op | source)
XLA Modules:
  0.0 46.5 jit_solution(15502855554404015526)
XLA Ops:
  1.9 42.9 %shard_map.86 = (bf16[256,256]{1,0:T(8,128)(2,1)}, bf16[3,64,256]{2,1,0:T(8,128)(2,1)}) custom-call(s32[1]{0:T(128)S(6)} %copy.9.start_ref, s32[1,1]{1,0:T(1,128)S(6)} %copy.10.len_ref, bf16[256,256]{1,0:T(8,128)(2,1)} %bitcast.5, bf16[256,256]{1,0:T(8,128)(2,1)} %bitcast.6, f32[1,256]{1,0:T(1,128)} %rate_ref.1, bf16[256,256]{1,0:T(8,128)(2,1)} %bitcast.7, ...), custom_call_target="tpu_custom_call" | custom-call | tf_op jit(solution)/shard_map/pallas_call | solution.py:300
  44.8 1.7 %shard_map.87 = (bf16[256,256]{1,0:T(8,128)(2,1)}, f32[3,64,256]{2,1,0:T(8,128)}) custom-call(bf16[256,256]{1,0:T(8,128)(2,1)} %get-tuple-element.6.out_ref, bf16[3,64,256]{2,1,0:T(8,128)(2,1)} %get-tuple-element.7.final_ref), custom_call_target="tpu_custom_call" | custom-call | tf_op jit(solution)/shard_map/pallas_call | solution.py:337

commit v2 on v1

--- a/solution.py
+++ b/solution.py
@@ -63,32 +63,29 @@
 
 def kernel(
     n, m, nb, start_ref, len_ref, key_ref, value_ref, rate_ref, q_ref, init_ref, out_ref, final_ref,
-    kv, queue, outs, halves, state, root, grad, fin, val_v, rate_v, q_v, nv_v,
-    in_sem, kv_send, kv_recv, q_send, q_recv, h_send, h_recv, o_send, o_recv, f_send, f_recv,
+    kv, queue, outs, halves, state, root, grad, fin, val_v, rate_v, q_v, nv_v, first_v, len_v,
+    in_sem, kv_send, kv_recv, pass_send, q_send, q_recv, h_send, h_recv, o_send, o_recv, f_send, f_recv,
     go, qgo,
 ):
     z, x, b = lax.axis_index("seq"), lax.axis_index("inner"), lax.axis_index("batch")
     tok, head = value_ref.shape
     rows = final_ref.shape[1]
 
-    def master_of(v):
-        return lax.rem(v, m), (n // 2) * (1 - lax.rem(v, 2))
+    def home(v):
+        return (n // 2) * (1 - lax.rem(v, 2))
 
     other = lax.rem(b + 1, nb)
     served = lax.rem(b + nb - 1, nb)
-    mx, mz = master_of(b)
-    sx, sz = master_of(served)
-    is_master = (x == mx) & (z == mz)
+    mz, sz = home(b), home(served)
+    is_master, is_server = z == mz, z == sz
     is_source = jnp.logical_not(is_master)
-    is_server = (x == sx) & (z == sz)
-    master = {"inner": mx, "seq": mz}
-    server = {"inner": mx, "seq": mz, "batch": other}
+    upper = z > mz
 
     def same_side(lower):
         return (lower >= 0) & (lower + 1 < n) & ((lower + 1 < mz) | (lower > mz))
 
     has_next, has_prev = same_side(z), same_side(z - 1)
-    upper = z > mz
+    twins = [lax.rem(x + d, m) for d in range(1, m)]
 
     barrier = pltpu.get_barrier_semaphore()
 
@@ -97,18 +94,16 @@
 
     @pl.when(is_master)
     def _():
-        @pl.loop(0, n)
-        def _(c):
-            for r in range(m):
-                pl.when((c != mz) | (r != mx))(lambda: greet({"seq": c, "inner": r}))
-        greet(server)
+        for r in twins:
+            greet({"inner": r})
+        for r in range(m):
+            greet({"inner": r, "batch": other})
 
     @pl.when(is_server)
     def _():
         @pl.loop(0, n)
         def _(c):
-            for r in range(m):
-                greet({"seq": c, "inner": r, "batch": served})
+            greet({"seq": c, "batch": served})
 
     pl.when(has_prev)(lambda: greet({"seq": z - 1}))
 
@@ -119,71 +114,87 @@
     get_rate = fetch(rate_ref, rate_v, 1)
     get_q = fetch(q_ref, q_v, 2)
     get_init = fetch(init_ref, state, 3)
-    get_key = fetch(key_ref, kv.at[mz, mx, 0], 4)
+    get_key = fetch(key_ref, kv.at[mz, x, 0], 4)
+    get_first = fetch(start_ref, first_v, 5)
+    get_len = fetch(len_ref, len_v, 6)
+    get_first.start()
+    get_len.start()
+    get_rate.start()
     get_val.start()
-    get_rate.start()
     pl.when(is_master)(get_key.start)
     pl.when(z == 0)(get_q.start)
     pl.when((z == 0) | is_master)(get_init.start)
 
     within = lax.broadcasted_iota(jnp.int32, (1, tok), 1) + x * tok
     position = within + z * (tok * m)
-    valid = ((position >= start_ref[0]) & (within < len_ref[0, 0])).astype(F32)
-    get_rate.wait()
-    weight = rate_v[...] * valid
     eye = lax.broadcasted_iota(jnp.int32, (tok, tok), 0) == lax.broadcasted_iota(
         jnp.int32, (tok, tok), 1
     )
+    get_first.wait()
+    get_len.wait()
+    get_rate.wait()
+    valid = ((position >= first_v[...]) & (within < len_v[...])).astype(F32)
+    weight = rate_v[...] * valid
     column = jnp.sum(jnp.where(eye, weight, 0.0), axis=1, keepdims=True)
     get_val.wait()
-    neg = (-(column * val_v[...].astype(F32))).astype(BF16)
-    nv_v[...] = neg
+    nv_v[...] = (-(column * val_v[...].astype(F32))).astype(BF16)
 
     pl.semaphore_wait(
         barrier,
-        1 + is_source.astype(jnp.int32) + is_server.astype(jnp.int32) + has_next.astype(jnp.int32),
+        1
+        + is_master.astype(jnp.int32) * (m - 1)
+        + is_server.astype(jnp.int32) * m
+        + has_next.astype(jnp.int32),
     )
 
     def copy(src, dst, send, recv, where):
         return pltpu.make_async_remote_copy(src, dst, send, recv, where, MESH)
 
-    give_k = copy(key_ref, kv.at[z, x, 0], kv_send.at[0], kv_recv.at[z, x, 0], master)
-    give_nv = copy(nv_v, kv.at[z, x, 1], kv_send.at[1], kv_recv.at[z, x, 1], master)
-    give_q = copy(q_ref, queue.at[z, x], q_send, q_recv.at[z, x], server)
-
-    def take(c, r, j):
-        return copy(kv.at[c, r, j], kv.at[c, r, j], kv_send.at[j], kv_recv.at[c, r, j], master)
+    def give(i, where, slot):
+        src = key_ref if i == 0 else nv_v
+        return copy(src, kv.at[z, x, i], kv_send.at[slot, i], kv_recv.at[z, x, i], where)
+
+    def take(c, r, i):
+        block = kv.at[c, r, i]
+        return copy(block, block, kv_send.at[0, i], kv_recv.at[c, r, i], {"seq": mz})
+
+    def forward(c, i, r, slot):
+        block = kv.at[c, x, i]
+        where = {"inner": r, "batch": served}
+        return copy(block, block, pass_send.at[c, i, slot], kv_recv.at[c, x, i], where)
+
+    server = {"seq": mz, "batch": other}
+    give_q = copy(q_ref, queue.at[z], q_send, q_recv.at[z], server)
 
     def give_half(c):
         return copy(halves.at[c], halves.at[c], h_send.at[c], h_recv.at[c], server)
 
-    def give_out(c, r):
-        where = {"seq": c, "inner": r, "batch": served}
-        return copy(outs.at[c, r], out_ref, o_send.at[c, r], o_recv, where)
-
-    def give_final(c, r, i):
+    def give_out(c):
+        where = {"seq": c, "batch": served}
+        return copy(outs.at[c], out_ref, o_send.at[c], o_recv, where)
+
+    def give_final(c, i):
         mine = pl.ds(pl.multiple_of(c * rows, rows), rows)
-        where = {"seq": c, "inner": r}
-        return copy(fin.at[i, mine], final_ref.at[i], f_send.at[c, r, i], f_recv.at[i], where)
+        return copy(fin.at[i, mine], final_ref.at[i], f_send.at[c, i], f_recv.at[i], {"seq": c})
+
+    def call_next():
+        pl.semaphore_signal(go, inc=1, device_id={"seq": z + 1}, device_id_type=MESH)
 
     @pl.when(is_source)
     def _():
         pl.when(has_prev)(lambda: pl.semaphore_wait(go, 1))
-        give_k.start()
-        give_nv.start()
-
-        @pl.when(has_next)
-        def _():
-            pl.semaphore_signal(go, inc=1, device_id={"seq": z + 1}, device_id_type=MESH)
-            pl.when(upper)(lambda: pl.semaphore_wait(qgo, 1))
-
-    @pl.when(z > 0)
-    def _():
-        give_q.start()
-
-        @pl.when(has_prev & upper)
-        def _():
-            pl.semaphore_signal(qgo, inc=1, device_id={"seq": z - 1}, device_id_type=MESH)
+        for i in range(2):
+            give(i, server, 0).start()
+        give(0, server, 0).wait_send()
+        pl.when(has_next)(call_next)
+        pl.when((z > 0) & jnp.logical_not(upper))(give_q.start)
+
+    @pl.when(is_master)
+    def _():
+        for d, r in enumerate(twins):
+            for i in range(2):
+                give(i, {"inner": r}, d).start()
+        pl.when(z > 0)(give_q.start)
 
     pl.when((z == 0) | is_master)(get_init.wait)
 
@@ -200,19 +211,39 @@
         root[i] = total * lax.rsqrt(total)
         return scale
 
+    @pl.when(is_server)
+    def _():
+        @pl.loop(0, n)
+        def _(c):
+            @pl.when(c != sz)
+            def _():
+                for i in range(2):
+                    take(c, x, i).wait_recv()
+                    for d, r in enumerate(twins + [x]):
+                        forward(c, i, r, d).start()
+
+    @pl.when(is_source & upper)
+    def _():
+        pl.when(has_next)(lambda: pl.semaphore_wait(qgo, 1))
+        give_q.start()
+
+        @pl.when(has_prev)
+        def _():
+            pl.semaphore_signal(qgo, inc=1, device_id={"seq": z - 1}, device_id_type=MESH)
+
     @pl.when(is_master)
     def _():
         for i in range(3):
             w = state[i]
             root[i] = jnp.sqrt(jnp.sum(w * w, axis=0, keepdims=True) + column_eps)
-        kv[mz, mx, 1] = nv_v[...]
+        kv[mz, x, 1] = nv_v[...]
         get_key.wait()
 
         @pl.loop(0, n)
         def _(c):
             for r in range(m):
-                for j in range(2):
-                    pl.when((c != mz) | (r != mx))(lambda: take(c, r, j).wait_recv())
+                for i in range(2):
+                    pl.when((c != mz) | (r != x))(lambda: take(c, r, i).wait_recv())
             scales = [sums(i) for i in range(3)]
             ws = [state[i].astype(BF16) for i in range(3)]
             k = kv[c, :, 0].reshape(m * tok, head)
@@ -234,48 +265,50 @@
         @pl.loop(0, n)
         def _(d):
             c = n - 1 - d
-            for r in range(m):
-                for i in range(3):
-                    pl.when((c != mz) | (r != mx))(lambda: give_final(c, r, i).start())
+            for i in range(3):
+                pl.when(c != mz)(lambda: give_final(c, i).start())
 
         mine = pl.ds(pl.multiple_of(z * rows, rows), rows)
         final_ref[...] = fin[:, mine, :]
 
         @pl.loop(0, n)
         def _(c):
-            for r in range(m):
-                for i in range(3):
-                    pl.when((c != mz) | (r != mx))(lambda: give_final(c, r, i).wait_send())
+            for i in range(3):
+                pl.when(c != mz)(lambda: give_final(c, i).wait_send())
             pl.when(c > 0)(lambda: give_half(c).wait_send())
+        for d, r in enumerate(twins):
+            for i in range(2):
+                give(i, {"inner": r}, d).wait_send()
 
     @pl.when(is_server)
     def _():
         @pl.loop(1, n)
         def _(c):
-            for r in range(m):
-                copy(queue.at[c, r], queue.at[c, r], q_send, q_recv.at[c, r], server).wait_recv()
+            copy(queue.at[c], queue.at[c], q_send, q_recv.at[c], server).wait_recv()
             give_half(c).wait_recv()
-            ws = [halves[c, i] for i in range(3)]
-            for r in range(m):
-                outs[c, r] = apply_net(queue[c, r], *ws)
-                give_out(c, r).start()
-
-        @pl.loop(1, n)
-        def _(c):
-            for r in range(m):
-                give_out(c, r).wait_send()
+            outs[c] = apply_net(queue[c], *[halves[c, i] for i in range(3)])
+            give_out(c).start()
+
+        @pl.loop(0, n)
+        def _(c):
+            pl.when(c > 0)(lambda: give_out(c).wait_send())
+
+            @pl.when(c != sz)
+            def _():
+                for i in range(2):
+                    for d, r in enumerate(twins + [x]):
+                        forward(c, i, r, d).wait_send()
 
     @pl.when(is_source)
     def _():
-        give_k.wait_send()
-        give_nv.wait_send()
+        give(1, server, 0).wait_send()
         for i in range(3):
-            give_final(0, 0, i).wait_recv()
+            give_final(0, i).wait_recv()
 
     @pl.when(z > 0)
     def _():
         give_q.wait_send()
-        give_out(0, 0).wait_recv()
+        give_out(0).wait_recv()
 
 
 def finish(out_ref, final_ref, out_hbm, final_hbm, wide, sem):
@@ -294,7 +327,6 @@
     hidden = init_weights.shape[2]
     rows = init_weights.shape[1] // n
     vm = pl.BlockSpec(memory_space=pltpu.VMEM)
-    sm = pl.BlockSpec(memory_space=pltpu.SMEM)
     hbm = pl.BlockSpec(memory_space=pl.ANY)
     dma = pltpu.SemaphoreType.DMA
     out, final = pl.pallas_call(
@@ -303,12 +335,12 @@
             jax.ShapeDtypeStruct((tok, head), BF16),
             jax.ShapeDtypeStruct((3, rows, hidden), BF16),
         ),
-        in_specs=[sm, sm, hbm, hbm, hbm, hbm, hbm],
+        in_specs=[hbm] * 7,
         out_specs=(vm, vm),
         scratch_shapes=[
             pltpu.VMEM((n, m, 2, tok, head), BF16),
-            pltpu.VMEM((n, m, tok, head), BF16),
-            pltpu.VMEM((n, m, tok, head), BF16),
+            pltpu.VMEM((n, tok, head), BF16),
+            pltpu.VMEM((n, tok, head), BF16),
             pltpu.VMEM((n,) + init_weights.shape, BF16),
             pltpu.VMEM(init_weights.shape, F32),
             pltpu.VMEM((3, 1, hidden), F32),
@@ -318,22 +350,25 @@
             pltpu.VMEM((1, tok), F32),
             pltpu.VMEM((tok, head), BF16),
             pltpu.VMEM((tok, head), BF16),
-            dma((5,)),
-            dma((2,)),
+            pltpu.VMEM((1, 1), jnp.int32),
+            pltpu.VMEM((1, 1), jnp.int32),
+            dma((7,)),
+            dma((max(m - 1, 1), 2)),
             dma((n, m, 2)),
+            dma((n, 2, m)),
             dma(()),
-            dma((n, m)),
             dma((n,)),
             dma((n,)),
-            dma((n, m)),
+            dma((n,)),
+            dma((n,)),
             dma(()),
-            dma((n, m, 3)),
+            dma((n, 3)),
             dma((3,)),
             pltpu.SemaphoreType.REGULAR,
             pltpu.SemaphoreType.REGULAR,
         ],
         compiler_params=pltpu.CompilerParams(collective_id=0, has_side_effects=True),
-    )(video_start, span_len, keys[0], values[0], rates, queries[0], init_weights)
+    )(video_start[None], span_len, keys[0], values[0], rates, queries[0], init_weights)
     out, final = pl.pallas_call(
         finish,
         out_shape=(

time: 46.7 us -> 34.7 us (0.74)
  the two profiles are of different devices: /device:TPU:15 before, /device:TPU:0 now
where the time goes in v2:
time: 34.7 us; the launch traced here: 34.5 us
  Pallas kernels  32.6 us (94%)
  between operations  1.93 us (6%)
    pallas_call x1, Pallas kernels, per_device(): pl.pallas_call(functools.partial(kernel, n, m, nb), out_shape=(jax.ShapeD...  30.9 us
    pallas_call x1, Pallas kernels, per_device(): pl.pallas_call(finish, out_shape=(jax.ShapeDtypeStruct((tok, head), BF16)...  1.69 us

profile of v2, /device:TPU:0, one launch (start us, length us, event | category | flops | bytes accessed | tf_op | source)
XLA Modules:
  0.0 34.5 jit_solution(12427462668240053694)
XLA Ops:
  1.9 30.9 %shard_map.86 = (bf16[256,256]{1,0:T(8,128)(2,1)}, bf16[3,64,256]{2,1,0:T(8,128)(2,1)}) custom-call(s32[1,1]{1,0:T(1,128)} %bitcast.6.start_ref, s32[1,1]{1,0:T(1,128)S(6)} %copy.10.len_ref, bf16[256,256]{1,0:T(8,128)(2,1)} %bitcast.7, bf16[256,256]{1,0:T(8,128)(2,1)} %bitcast.8, f32[1,256]{1,0:T(1,128)} %rate_ref.1, bf16[256,256]{1,0:T(8,128)(2,1)} %bitcast.9, ...), custom_call_target="tpu_custom_call" | custom-call | tf_op jit(solution)/shard_map/pallas_call | solution.py:332
  32.8 1.7 %shard_map.87 = (bf16[256,256]{1,0:T(8,128)(2,1)}, f32[3,64,256]{2,1,0:T(8,128)}) custom-call(bf16[256,256]{1,0:T(8,128)(2,1)} %get-tuple-element.6.out_ref, bf16[3,64,256]{2,1,0:T(8,128)(2,1)} %get-tuple-element.7.final_ref), custom_call_target="tpu_custom_call" | custom-call | tf_op jit(solution)/shard_map/pallas_call | solution.py:372

commit v3 on v2

--- a/solution.py
+++ b/solution.py
@@ -8,6 +8,8 @@
 from jax.sharding import PartitionSpec as P
 
 NS_STEPS = 5
+CHUNKS = 2
+CALL_AFTER = 1
 MESH = pl.DeviceIdType.MESH
 step_size = 0.1
 norm_eps = 1e-07
@@ -133,7 +135,7 @@
     get_first.wait()
     get_len.wait()
     get_rate.wait()
-    valid = ((position >= first_v[...]) & (within < len_v[...])).astype(F32)
+    valid = ((position >= first_v[0]) & (within < len_v[0, 0])).astype(F32)
     weight = rate_v[...] * valid
     column = jnp.sum(jnp.where(eye, weight, 0.0), axis=1, keepdims=True)
     get_val.wait()
@@ -150,18 +152,23 @@
     def copy(src, dst, send, recv, where):
         return pltpu.make_async_remote_copy(src, dst, send, recv, where, MESH)
 
-    def give(i, where, slot):
-        src = key_ref if i == 0 else nv_v
-        return copy(src, kv.at[z, x, i], kv_send.at[slot, i], kv_recv.at[z, x, i], where)
-
-    def take(c, r, i):
-        block = kv.at[c, r, i]
-        return copy(block, block, kv_send.at[0, i], kv_recv.at[c, r, i], {"seq": mz})
-
-    def forward(c, i, r, slot):
-        block = kv.at[c, x, i]
+    pieces = 2 * CHUNKS
+    part = tok // CHUNKS
+
+    def piece(c, r, j):
+        return kv.at[c, r, j // CHUNKS, pl.ds(j % CHUNKS * part, part)]
+
+    def give(j, where, slot):
+        src = (key_ref if j < CHUNKS else nv_v).at[pl.ds(j % CHUNKS * part, part)]
+        return copy(src, piece(z, x, j), kv_send.at[slot, j], kv_recv.at[z, x, j], where)
+
+    def take(c, r, j):
+        return copy(piece(c, r, j), piece(c, r, j), kv_send.at[0, j], kv_recv.at[c, r, j], {"seq": mz})
+
+    def forward(c, j, r, slot):
         where = {"inner": r, "batch": served}
-        return copy(block, block, pass_send.at[c, i, slot], kv_recv.at[c, x, i], where)
+        block = piece(c, x, j)
+        return copy(block, block, pass_send.at[c, j, slot], kv_recv.at[c, x, j], where)
 
     server = {"seq": mz, "batch": other}
     give_q = copy(q_ref, queue.at[z], q_send, q_recv.at[z], server)
@@ -183,17 +190,18 @@
     @pl.when(is_source)
     def _():
         pl.when(has_prev)(lambda: pl.semaphore_wait(go, 1))
-        for i in range(2):
-            give(i, server, 0).start()
-        give(0, server, 0).wait_send()
+        for j in range(pieces):
+            give(j, server, 0).start()
+        for j in range(CALL_AFTER):
+            give(j, server, 0).wait_send()
         pl.when(has_next)(call_next)
         pl.when((z > 0) & jnp.logical_not(upper))(give_q.start)
 
     @pl.when(is_master)
     def _():
         for d, r in enumerate(twins):
-            for i in range(2):
-                give(i, {"inner": r}, d).start()
+            for j in range(pieces):
+                give(j, {"inner": r}, d).start()
         pl.when(z > 0)(give_q.start)
 
     pl.when((z == 0) | is_master)(get_init.wait)
@@ -217,10 +225,10 @@
         def _(c):
             @pl.when(c != sz)
             def _():
-                for i in range(2):
-                    take(c, x, i).wait_recv()
+                for j in range(pieces):
+                    take(c, x, j).wait_recv()
                     for d, r in enumerate(twins + [x]):
-                        forward(c, i, r, d).start()
+                        forward(c, j, r, d).start()
 
     @pl.when(is_source & upper)
     def _():
@@ -242,20 +250,20 @@
         @pl.loop(0, n)
         def _(c):
             for r in range(m):
-                for i in range(2):
-                    pl.when((c != mz) | (r != x))(lambda: take(c, r, i).wait_recv())
+                for j in range(pieces):
+                    pl.when((c != mz) | (r != x))(lambda: take(c, r, j).wait_recv())
             scales = [sums(i) for i in range(3)]
             ws = [state[i].astype(BF16) for i in range(3)]
             k = kv[c, :, 0].reshape(m * tok, head)
             nv = kv[c, :, 1].reshape(m * tok, head)
-            for i, g in enumerate(span_grads(k, nv, ws, scales)):
-                grad[i] = g
             for i in range(3):
                 w = state[i] * scales[i]
                 state[i] = w
                 halves[c, i] = w.astype(BF16)
+            for i, g in enumerate(span_grads(k, nv, ws, scales)):
+                grad[i] = g
+            pl.when(c > 0)(lambda: give_half(c).start())
             ys = newton([grad[i] for i in range(3)])
-            pl.when(c > 0)(lambda: give_half(c).start())
             for i in range(3):
                 state[i] = state[i] + (step_size / half_root) * ys[i]
 
@@ -264,7 +272,7 @@
 
         @pl.loop(0, n)
         def _(d):
-            c = n - 1 - d
+            c = jnp.where(mz < n // 2, n - 1 - d, d)
             for i in range(3):
                 pl.when(c != mz)(lambda: give_final(c, i).start())
 
@@ -277,8 +285,8 @@
                 pl.when(c != mz)(lambda: give_final(c, i).wait_send())
             pl.when(c > 0)(lambda: give_half(c).wait_send())
         for d, r in enumerate(twins):
-            for i in range(2):
-                give(i, {"inner": r}, d).wait_send()
+            for j in range(pieces):
+                give(j, {"inner": r}, d).wait_send()
 
     @pl.when(is_server)
     def _():
@@ -295,13 +303,14 @@
 
             @pl.when(c != sz)
             def _():
-                for i in range(2):
+                for j in range(pieces):
                     for d, r in enumerate(twins + [x]):
-                        forward(c, i, r, d).wait_send()
+                        forward(c, j, r, d).wait_send()
 
     @pl.when(is_source)
     def _():
-        give(1, server, 0).wait_send()
+        for j in range(CALL_AFTER, pieces):
+            give(j, server, 0).wait_send()
         for i in range(3):
             give_final(0, i).wait_recv()
 
@@ -332,10 +341,10 @@
     out, final = pl.pallas_call(
         functools.partial(kernel, n, m, nb),
         out_shape=(
-            jax.ShapeDtypeStruct((tok, head), BF16),
-            jax.ShapeDtypeStruct((3, rows, hidden), BF16),
+            pltpu.VMEM((tok, head), BF16),
+            pltpu.VMEM((3, rows, hidden), BF16),
         ),
-        in_specs=[hbm] * 7,
+        in_specs=[pl.BlockSpec(memory_space=pltpu.HBM)] * 7,
         out_specs=(vm, vm),
         scratch_shapes=[
             pltpu.VMEM((n, m, 2, tok, head), BF16),
@@ -350,12 +359,12 @@
             pltpu.VMEM((1, tok), F32),
             pltpu.VMEM((tok, head), BF16),
             pltpu.VMEM((tok, head), BF16),
-            pltpu.VMEM((1, 1), jnp.int32),
-            pltpu.VMEM((1, 1), jnp.int32),
+            pltpu.SMEM((1,), jnp.int32),
+            pltpu.SMEM((1, 1), jnp.int32),
             dma((7,)),
-            dma((max(m - 1, 1), 2)),
-            dma((n, m, 2)),
-            dma((n, 2, m)),
+            dma((max(m - 1, 1), 2 * CHUNKS)),
+            dma((n, m, 2 * CHUNKS)),
+            dma((n, 2 * CHUNKS, m)),
             dma(()),
             dma((n,)),
             dma((n,)),
@@ -368,7 +377,7 @@
             pltpu.SemaphoreType.REGULAR,
         ],
         compiler_params=pltpu.CompilerParams(collective_id=0, has_side_effects=True),
-    )(video_start[None], span_len, keys[0], values[0], rates, queries[0], init_weights)
+    )(video_start, span_len, keys[0], values[0], rates, queries[0], init_weights)
     out, final = pl.pallas_call(
         finish,
         out_shape=(
@@ -378,7 +387,7 @@
         in_specs=[vm, vm],
         out_specs=(hbm, hbm),
         scratch_shapes=[pltpu.VMEM((3, rows, hidden), F32), dma((2,))],
-    )(out, final)
+    )(*[pltpu.with_memory_space_constraint(a, pltpu.VMEM) for a in (out, final)])
     return out[None], final[None]
 
 

time: 34.7 us -> 31.5 us (0.908)
  Pallas kernels: 32.6 us -> 29.4 us
    pallas_call x1, Pallas kernels: 30.9 us -> 28.6 us  [per_device(): pl.pallas_call(functools.partial(kernel, n, m, nb), out_shape=(pltpu.VMEM...]
    pallas_call x1, Pallas kernels: 1.69 us -> 0.74 us  [per_device(): pl.pallas_call(finish, out_shape=(jax.ShapeDtypeStruct((tok, head), BF16)...]
where the time goes in v3:
time: 31.5 us; the launch traced here: 31.3 us
  Pallas kernels  29.4 us (93%)
  between operations  1.93 us (6%)
    pallas_call x1, Pallas kernels, per_device(): pl.pallas_call(functools.partial(kernel, n, m, nb), out_shape=(pltpu.VMEM...  28.6 us
    pallas_call x1, Pallas kernels, per_device(): pl.pallas_call(finish, out_shape=(jax.ShapeDtypeStruct((tok, head), BF16)...  0.74 us

profile of v3, /device:TPU:0, one launch (start us, length us, event | category | flops | bytes accessed | tf_op | source)
XLA Modules:
  0.0 31.3 jit_solution(13837625472357634896)
XLA Ops:
  1.9 28.6 %shard_map.86 = (bf16[256,256]{1,0:T(8,128)(2,1)S(1)}, bf16[3,64,256]{2,1,0:T(8,128)(2,1)S(1)}) custom-call(s32[1]{0:T(128)S(6)} %copy.9.start_ref, s32[1,1]{1,0:T(1,128)S(6)} %copy.10.len_ref, bf16[256,256]{1,0:T(8,128)(2,1)} %bitcast.5, bf16[256,256]{1,0:T(8,128)(2,1)} %bitcast.6, f32[1,256]{1,0:T(1,128)} %rate_ref.1, bf16[256,256]{1,0:T(8,128)(2,1)} %bitcast.7, ...), custom_call_target="tpu_custom_call" | custom-call | tf_op jit(solution)/shard_map/pallas_call | solution.py:341
  30.6 0.7 %shard_map.87 = (bf16[256,256]{1,0:T(8,128)(2,1)}, f32[3,64,256]{2,1,0:T(8,128)}) custom-call(bf16[256,256]{1,0:T(8,128)(2,1)S(1)} %get-tuple-element.6.out_ref, bf16[3,64,256]{2,1,0:T(8,128)(2,1)S(1)} %get-tuple-element.7.final_ref), custom_call_target="tpu_custom_call" | custom-call | tf_op jit(solution)/shard_map/pallas_call | solution.py:381

commit v4 on v3

--- a/solution.py
+++ b/solution.py
@@ -10,6 +10,7 @@
 NS_STEPS = 5
 CHUNKS = 2
 CALL_AFTER = 1
+QUERY_AFTER = 2
 MESH = pl.DeviceIdType.MESH
 step_size = 0.1
 norm_eps = 1e-07
@@ -65,8 +66,8 @@
 
 def kernel(
     n, m, nb, start_ref, len_ref, key_ref, value_ref, rate_ref, q_ref, init_ref, out_ref, final_ref,
-    kv, queue, outs, halves, state, root, grad, fin, val_v, rate_v, q_v, nv_v, first_v, len_v,
-    in_sem, kv_send, kv_recv, pass_send, q_send, q_recv, h_send, h_recv, o_send, o_recv, f_send, f_recv,
+    kv, queue, outs, halves, state, root, grad, fin, val_v, rate_v, q_v, nv_v,
+    in_sem, kv_send, twin_send, part_recv, kv_recv, pass_send, q_send, q_recv, h_send, h_recv, o_send, o_recv, f_send, f_recv,
     go, qgo,
 ):
     z, x, b = lax.axis_index("seq"), lax.axis_index("inner"), lax.axis_index("batch")
@@ -108,6 +109,10 @@
             greet({"seq": c, "batch": served})
 
     pl.when(has_prev)(lambda: greet({"seq": z - 1}))
+    many = mz + 2 < n
+    is_first, is_last = upper & many & (z == mz + 1), upper & many & (z == n - 1)
+    holds_last = upper & many & (z == n - 2)
+    pl.when(is_first)(lambda: greet({"seq": n - 1}))
 
     def fetch(src, dst, i):
         return pltpu.make_async_copy(src, dst, in_sem.at[i])
@@ -117,10 +122,6 @@
     get_q = fetch(q_ref, q_v, 2)
     get_init = fetch(init_ref, state, 3)
     get_key = fetch(key_ref, kv.at[mz, x, 0], 4)
-    get_first = fetch(start_ref, first_v, 5)
-    get_len = fetch(len_ref, len_v, 6)
-    get_first.start()
-    get_len.start()
     get_rate.start()
     get_val.start()
     pl.when(is_master)(get_key.start)
@@ -132,10 +133,8 @@
     eye = lax.broadcasted_iota(jnp.int32, (tok, tok), 0) == lax.broadcasted_iota(
         jnp.int32, (tok, tok), 1
     )
-    get_first.wait()
-    get_len.wait()
     get_rate.wait()
-    valid = ((position >= first_v[0]) & (within < len_v[0, 0])).astype(F32)
+    valid = ((position >= start_ref[0]) & (within < len_ref[0, 0])).astype(F32)
     weight = rate_v[...] * valid
     column = jnp.sum(jnp.where(eye, weight, 0.0), axis=1, keepdims=True)
     get_val.wait()
@@ -146,7 +145,8 @@
         1
         + is_master.astype(jnp.int32) * (m - 1)
         + is_server.astype(jnp.int32) * m
-        + has_next.astype(jnp.int32),
+        + has_next.astype(jnp.int32)
+        + is_last.astype(jnp.int32),
     )
 
     def copy(src, dst, send, recv, where):
@@ -158,31 +158,52 @@
     def piece(c, r, j):
         return kv.at[c, r, j // CHUNKS, pl.ds(j % CHUNKS * part, part)]
 
-    def give(j, where, slot):
-        src = (key_ref if j < CHUNKS else nv_v).at[pl.ds(j % CHUNKS * part, part)]
-        return copy(src, piece(z, x, j), kv_send.at[slot, j], kv_recv.at[z, x, j], where)
-
-    def take(c, r, j):
-        return copy(piece(c, r, j), piece(c, r, j), kv_send.at[0, j], kv_recv.at[c, r, j], {"seq": mz})
-
-    def forward(c, j, r, slot):
+    def own_piece(j):
+        return (key_ref if j < CHUNKS else nv_v).at[pl.ds(j % CHUNKS * part, part)]
+
+    def give(j):
+        send = kv_send.at[min(j, CHUNKS)]
+        return copy(own_piece(j), piece(z, x, j), send, part_recv.at[z, j], server)
+
+    def sent(j):
+        return give(j) if j < CHUNKS else copy(nv_v, nv_v, kv_send.at[j], part_recv.at[z, j], server)
+
+    def give_twin(j, d):
+        where = {"inner": twins[d]}
+        return copy(own_piece(j), piece(z, x, j), twin_send.at[d], kv_recv.at[z, x], where)
+
+    def take_piece(c, j):
+        return copy(piece(c, x, j), piece(c, x, j), pass_send, part_recv.at[c, j], server)
+
+    def take(c, r, send=None):
+        block = kv.at[c, r]
+        return copy(block, block, twin_send.at[0] if send is None else send, kv_recv.at[c, r], server)
+
+    def forward(c, j, r):
         where = {"inner": r, "batch": served}
         block = piece(c, x, j)
-        return copy(block, block, pass_send.at[c, j, slot], kv_recv.at[c, x, j], where)
+        return copy(block, block, pass_send, kv_recv.at[c, x], where)
 
     server = {"seq": mz, "batch": other}
-    give_q = copy(q_ref, queue.at[z], q_send, q_recv.at[z], server)
+
+    def give_query(h):
+        half = pl.ds(h * (tok // 2), tok // 2)
+        return copy(q_ref.at[half], queue.at[z, half], q_send.at[h], q_recv.at[z], server)
+
+    def give_queries():
+        for h in range(2):
+            give_query(h).start()
 
     def give_half(c):
-        return copy(halves.at[c], halves.at[c], h_send.at[c], h_recv.at[c], server)
+        return copy(halves.at[c], halves.at[c], h_send, h_recv.at[c], server)
 
     def give_out(c):
         where = {"seq": c, "batch": served}
-        return copy(outs.at[c], out_ref, o_send.at[c], o_recv, where)
+        return copy(outs.at[c], out_ref, o_send, o_recv, where)
 
     def give_final(c, i):
         mine = pl.ds(pl.multiple_of(c * rows, rows), rows)
-        return copy(fin.at[i, mine], final_ref.at[i], f_send.at[c, i], f_recv.at[i], {"seq": c})
+        return copy(fin.at[i, mine], final_ref.at[i], f_send, f_recv, {"seq": c})
 
     def call_next():
         pl.semaphore_signal(go, inc=1, device_id={"seq": z + 1}, device_id_type=MESH)
@@ -191,18 +212,18 @@
     def _():
         pl.when(has_prev)(lambda: pl.semaphore_wait(go, 1))
         for j in range(pieces):
-            give(j, server, 0).start()
+            give(j).start()
         for j in range(CALL_AFTER):
-            give(j, server, 0).wait_send()
+            sent(j).wait_send()
         pl.when(has_next)(call_next)
-        pl.when((z > 0) & jnp.logical_not(upper))(give_q.start)
+        pl.when((z > 0) & jnp.logical_not(upper))(give_queries)
 
     @pl.when(is_master)
     def _():
         for d, r in enumerate(twins):
             for j in range(pieces):
-                give(j, {"inner": r}, d).start()
-        pl.when(z > 0)(give_q.start)
+                give_twin(j, d).start()
+        pl.when(z > 0)(give_queries)
 
     pl.when((z == 0) | is_master)(get_init.wait)
 
@@ -226,18 +247,25 @@
             @pl.when(c != sz)
             def _():
                 for j in range(pieces):
-                    take(c, x, j).wait_recv()
-                    for d, r in enumerate(twins + [x]):
-                        forward(c, j, r, d).start()
+                    take_piece(c, j).wait_recv()
+                    for r in twins + [x]:
+                        forward(c, j, r).start()
+
+    def call_query(where):
+        pl.semaphore_signal(qgo, inc=1, device_id={"seq": where}, device_id_type=MESH)
 
     @pl.when(is_source & upper)
     def _():
-        pl.when(has_next)(lambda: pl.semaphore_wait(qgo, 1))
-        give_q.start()
-
-        @pl.when(has_prev)
+        @pl.when(is_last)
         def _():
-            pl.semaphore_signal(qgo, inc=1, device_id={"seq": z - 1}, device_id_type=MESH)
+            for j in range(CALL_AFTER, QUERY_AFTER):
+                sent(j).wait_send()
+            call_query(mz + 1)
+
+        pl.when(many)(lambda: pl.semaphore_wait(qgo, 1))
+        give_queries()
+        pl.when(holds_last)(lambda: give_query(0).wait_send())
+        pl.when(has_next)(lambda: call_query(z + 1))
 
     @pl.when(is_master)
     def _():
@@ -247,30 +275,38 @@
         kv[mz, x, 1] = nv_v[...]
         get_key.wait()
 
-        @pl.loop(0, n)
-        def _(c):
-            for r in range(m):
-                for j in range(pieces):
-                    pl.when((c != mz) | (r != x))(lambda: take(c, r, j).wait_recv())
+        def train(c, last):
+            for d in range(m):
+                r = lax.rem(x + d, m)
+                pl.when((c != mz) | (r != x))(lambda: take(c, r).wait_recv())
             scales = [sums(i) for i in range(3)]
             ws = [state[i].astype(BF16) for i in range(3)]
-            k = kv[c, :, 0].reshape(m * tok, head)
-            nv = kv[c, :, 1].reshape(m * tok, head)
             for i in range(3):
                 w = state[i] * scales[i]
                 state[i] = w
                 halves[c, i] = w.astype(BF16)
-            for i, g in enumerate(span_grads(k, nv, ws, scales)):
-                grad[i] = g
-            pl.when(c > 0)(lambda: give_half(c).start())
-            ys = newton([grad[i] for i in range(3)])
-            for i in range(3):
-                state[i] = state[i] + (step_size / half_root) * ys[i]
-
+            k = kv[c, :, 0].reshape(m * tok, head)
+            nv = kv[c, :, 1].reshape(m * tok, head)
+            grads = span_grads(k, nv, ws, scales)
+            if last:
+                for i in range(3):
+                    grad[i] = grads[i]
+                give_half(c).start()
+                grads = [grad[i] for i in range(3)]
+            for i, y in enumerate(newton(grads)):
+                state[i] = state[i] + (step_size / half_root) * y
+            if not last:
+                pl.when(c > 0)(lambda: give_half(c).start())
+
+        pl.loop(0, n - 1)(lambda c: train(c, False))
+        train(n - 1, True)
+
+        far = jnp.where(mz < n // 2, n - 1, 0)
         for i in range(3):
             fin[i] = (state[i] * sums(i)).astype(BF16)
-
-        @pl.loop(0, n)
+            give_final(far, i).start()
+
+        @pl.loop(1, n)
         def _(d):
             c = jnp.where(mz < n // 2, n - 1 - d, d)
             for i in range(3):
@@ -279,44 +315,39 @@
         mine = pl.ds(pl.multiple_of(z * rows, rows), rows)
         final_ref[...] = fin[:, mine, :]
 
-        @pl.loop(0, n)
-        def _(c):
-            for i in range(3):
-                pl.when(c != mz)(lambda: give_final(c, i).wait_send())
-            pl.when(c > 0)(lambda: give_half(c).wait_send())
+        rest = fin.at[:, pl.ds(0, (n - 1) * rows)]
+        copy(rest, rest, f_send, f_recv, server).wait_send()
+        rest = halves.at[pl.ds(1, n - 1)]
+        copy(rest, rest, h_send, h_recv.at[0], server).wait_send()
         for d, r in enumerate(twins):
-            for j in range(pieces):
-                give(j, {"inner": r}, d).wait_send()
+            take(z, x, twin_send.at[d]).wait_send()
 
     @pl.when(is_server)
     def _():
         @pl.loop(1, n)
         def _(c):
-            copy(queue.at[c], queue.at[c], q_send, q_recv.at[c], server).wait_recv()
+            copy(queue.at[c], queue.at[c], q_send.at[0], q_recv.at[c], server).wait_recv()
             give_half(c).wait_recv()
             outs[c] = apply_net(queue[c], *[halves[c, i] for i in range(3)])
             give_out(c).start()
 
-        @pl.loop(0, n)
-        def _(c):
-            pl.when(c > 0)(lambda: give_out(c).wait_send())
-
-            @pl.when(c != sz)
-            def _():
-                for j in range(pieces):
-                    for d, r in enumerate(twins + [x]):
-                        forward(c, j, r, d).wait_send()
+        rest = outs.at[pl.ds(1, n - 1)]
+        copy(rest, rest, o_send, o_recv, server).wait_send()
+        rest = kv.at[pl.ds(0, n - 1)]
+        copy(rest, rest, pass_send, kv_recv.at[0, 0], server).wait_send()
 
     @pl.when(is_source)
     def _():
-        for j in range(CALL_AFTER, pieces):
-            give(j, server, 0).wait_send()
-        for i in range(3):
-            give_final(0, i).wait_recv()
+        for j in range(CALL_AFTER, QUERY_AFTER):
+            pl.when(jnp.logical_not(is_last))(sent(j).wait_send)
+        for j in range(QUERY_AFTER, CHUNKS + 1):
+            sent(j).wait_send()
+        copy(final_ref, final_ref, f_send, f_recv, {"seq": 0}).wait_recv()
 
     @pl.when(z > 0)
     def _():
-        give_q.wait_send()
+        pl.when(jnp.logical_not(holds_last))(lambda: give_query(0).wait_send())
+        give_query(1).wait_send()
         give_out(0).wait_recv()
 
 
@@ -344,7 +375,7 @@
             pltpu.VMEM((tok, head), BF16),
             pltpu.VMEM((3, rows, hidden), BF16),
         ),
-        in_specs=[pl.BlockSpec(memory_space=pltpu.HBM)] * 7,
+        in_specs=[pl.BlockSpec(memory_space=pltpu.SMEM)] * 2 + [hbm] * 5,
         out_specs=(vm, vm),
         scratch_shapes=[
             pltpu.VMEM((n, m, 2, tok, head), BF16),
@@ -359,20 +390,20 @@
             pltpu.VMEM((1, tok), F32),
             pltpu.VMEM((tok, head), BF16),
             pltpu.VMEM((tok, head), BF16),
-            pltpu.SMEM((1,), jnp.int32),
-            pltpu.SMEM((1, 1), jnp.int32),
-            dma((7,)),
-            dma((max(m - 1, 1), 2 * CHUNKS)),
-            dma((n, m, 2 * CHUNKS)),
-            dma((n, 2 * CHUNKS, m)),
-            dma(()),
+            dma((5,)),
+            dma((CHUNKS + 1,)),
+            dma((max(m - 1, 1),)),
+            dma((n, 2 * CHUNKS)),
+            dma((n, m)),
+            dma(()),
+            dma((2,)),
             dma((n,)),
+            dma(()),
             dma((n,)),
-            dma((n,)),
-            dma((n,)),
-            dma(()),
-            dma((n, 3)),
-            dma((3,)),
+            dma(()),
+            dma(()),
+            dma(()),
+            dma(()),
             pltpu.SemaphoreType.REGULAR,
             pltpu.SemaphoreType.REGULAR,
         ],

time: 31.5 us -> 30.3 us (0.962)
  Pallas kernels: 29.4 us -> 28.1 us
    pallas_call x1, Pallas kernels: 28.6 us -> 27.4 us  [per_device(): pl.pallas_call(functools.partial(kernel, n, m, nb), out_shape=(pltpu.VMEM...]
where the time goes in v4:
time: 30.3 us; the launch traced here: 30.1 us
  Pallas kernels  28.1 us (93%)
  between operations  1.93 us (6%)
    pallas_call x1, Pallas kernels, per_device(): pl.pallas_call(functools.partial(kernel, n, m, nb), out_shape=(pltpu.VMEM...  27.4 us
    pallas_call x1, Pallas kernels, per_device(): pl.pallas_call(finish, out_shape=(jax.ShapeDtypeStruct((tok, head), BF16)...  0.74 us

profile of v4, /device:TPU:0, one launch (start us, length us, event | category | flops | bytes accessed | tf_op | source)
XLA Modules:
  0.0 30.1 jit_solution(4649932777148010875)
XLA Ops:
  1.9 27.4 %shard_map.86 = (bf16[256,256]{1,0:T(8,128)(2,1)S(1)}, bf16[3,64,256]{2,1,0:T(8,128)(2,1)S(1)}) custom-call(s32[1]{0:T(128)S(6)} %copy.9.start_ref, s32[1,1]{1,0:T(1,128)S(6)} %copy.10.len_ref, bf16[256,256]{1,0:T(8,128)(2,1)} %bitcast.5, bf16[256,256]{1,0:T(8,128)(2,1)} %bitcast.6, f32[1,256]{1,0:T(1,128)} %rate_ref.1, bf16[256,256]{1,0:T(8,128)(2,1)} %bitcast.7, ...), custom_call_target="tpu_custom_call" | custom-call | tf_op jit(solution)/shard_map/pallas_call | solution.py:372
  29.3 0.7 %shard_map.87 = (bf16[256,256]{1,0:T(8,128)(2,1)}, f32[3,64,256]{2,1,0:T(8,128)}) custom-call(bf16[256,256]{1,0:T(8,128)(2,1)S(1)} %get-tuple-element.6.out_ref, bf16[3,64,256]{2,1,0:T(8,128)(2,1)S(1)} %get-tuple-element.7.final_ref), custom_call_target="tpu_custom_call" | custom-call | tf_op jit(solution)/shard_map/pallas_call | solution.py:412

commit v5 on v4

--- a/solution.py
+++ b/solution.py
@@ -128,6 +128,86 @@
     pl.when(z == 0)(get_q.start)
     pl.when((z == 0) | is_master)(get_init.start)
 
+    pl.semaphore_wait(
+        barrier,
+        1
+        + is_master.astype(jnp.int32) * (m - 1)
+        + is_server.astype(jnp.int32) * m
+        + has_next.astype(jnp.int32)
+        + is_last.astype(jnp.int32),
+    )
+
+    def copy(src, dst, send, recv, where):
+        return pltpu.make_async_remote_copy(src, dst, send, recv, where, MESH)
+
+    pieces = 2 * CHUNKS
+    part = tok // CHUNKS
+
+    def piece(c, r, j):
+        return kv.at[c, r, j // CHUNKS, pl.ds(j % CHUNKS * part, part)]
+
+    def own_piece(j):
+        return (key_ref if j < CHUNKS else nv_v).at[pl.ds(j % CHUNKS * part, part)]
+
+    def give(j):
+        send = kv_send.at[min(j, CHUNKS)]
+        return copy(own_piece(j), piece(z, x, j), send, part_recv.at[z, j], server)
+
+    def sent(j):
+        return give(j) if j < CHUNKS else copy(nv_v, nv_v, kv_send.at[j], part_recv.at[z, j], server)
+
+    def give_twin(j, d):
+        where = {"inner": twins[d]}
+        return copy(own_piece(j), piece(z, x, j), twin_send.at[d], kv_recv.at[z, x], where)
+
+    def take_piece(c, j):
+        return copy(piece(c, x, j), piece(c, x, j), pass_send, part_recv.at[c, j], server)
+
+    def take(c, r, send=None):
+        block = kv.at[c, r]
+        return copy(block, block, twin_send.at[0] if send is None else send, kv_recv.at[c, r], server)
+
+    def forward(c, j, r):
+        where = {"inner": r, "batch": served}
+        block = piece(c, x, j)
+        return copy(block, block, pass_send, kv_recv.at[c, x], where)
+
+    server = {"seq": mz, "batch": other}
+
+    def give_query(h):
+        half = pl.ds(h * (tok // 2), tok // 2)
+        return copy(q_ref.at[half], queue.at[z, half], q_send.at[h], q_recv.at[z], server)
+
+    def give_queries():
+        for h in range(2):
+            give_query(h).start()
+
+    def give_half(c):
+        return copy(halves.at[c], halves.at[c], h_send, h_recv.at[c], server)
+
+    def give_out(c):
+        where = {"seq": c, "batch": served}
+        return copy(outs.at[c], out_ref, o_send, o_recv, where)
+
+    def give_final(c, i):
+        mine = pl.ds(pl.multiple_of(c * rows, rows), rows)
+        return copy(fin.at[i, mine], final_ref.at[i], f_send, f_recv, {"seq": c})
+
+    def call_next():
+        pl.semaphore_signal(go, inc=1, device_id={"seq": z + 1}, device_id_type=MESH)
+
+    @pl.when(is_source)
+    def _():
+        pl.when(has_prev)(lambda: pl.semaphore_wait(go, 1))
+        for j in range(CHUNKS):
+            give(j).start()
+
+    @pl.when(is_master)
+    def _():
+        for d, r in enumerate(twins):
+            for j in range(CHUNKS):
+                give_twin(j, d).start()
+
     within = lax.broadcasted_iota(jnp.int32, (1, tok), 1) + x * tok
     position = within + z * (tok * m)
     eye = lax.broadcasted_iota(jnp.int32, (tok, tok), 0) == lax.broadcasted_iota(
@@ -140,78 +220,9 @@
     get_val.wait()
     nv_v[...] = (-(column * val_v[...].astype(F32))).astype(BF16)
 
-    pl.semaphore_wait(
-        barrier,
-        1
-        + is_master.astype(jnp.int32) * (m - 1)
-        + is_server.astype(jnp.int32) * m
-        + has_next.astype(jnp.int32)
-        + is_last.astype(jnp.int32),
-    )
-
-    def copy(src, dst, send, recv, where):
-        return pltpu.make_async_remote_copy(src, dst, send, recv, where, MESH)
-
-    pieces = 2 * CHUNKS
-    part = tok // CHUNKS
-
-    def piece(c, r, j):
-        return kv.at[c, r, j // CHUNKS, pl.ds(j % CHUNKS * part, part)]
-
-    def own_piece(j):
-        return (key_ref if j < CHUNKS else nv_v).at[pl.ds(j % CHUNKS * part, part)]
-
-    def give(j):
-        send = kv_send.at[min(j, CHUNKS)]
-        return copy(own_piece(j), piece(z, x, j), send, part_recv.at[z, j], server)
-
-    def sent(j):
-        return give(j) if j < CHUNKS else copy(nv_v, nv_v, kv_send.at[j], part_recv.at[z, j], server)
-
-    def give_twin(j, d):
-        where = {"inner": twins[d]}
-        return copy(own_piece(j), piece(z, x, j), twin_send.at[d], kv_recv.at[z, x], where)
-
-    def take_piece(c, j):
-        return copy(piece(c, x, j), piece(c, x, j), pass_send, part_recv.at[c, j], server)
-
-    def take(c, r, send=None):
-        block = kv.at[c, r]
-        return copy(block, block, twin_send.at[0] if send is None else send, kv_recv.at[c, r], server)
-
-    def forward(c, j, r):
-        where = {"inner": r, "batch": served}
-        block = piece(c, x, j)
-        return copy(block, block, pass_send, kv_recv.at[c, x], where)
-
-    server = {"seq": mz, "batch": other}
-
-    def give_query(h):
-        half = pl.ds(h * (tok // 2), tok // 2)
-        return copy(q_ref.at[half], queue.at[z, half], q_send.at[h], q_recv.at[z], server)
-
-    def give_queries():
-        for h in range(2):
-            give_query(h).start()
-
-    def give_half(c):
-        return copy(halves.at[c], halves.at[c], h_send, h_recv.at[c], server)
-
-    def give_out(c):
-        where = {"seq": c, "batch": served}
-        return copy(outs.at[c], out_ref, o_send, o_recv, where)
-
-    def give_final(c, i):
-        mine = pl.ds(pl.multiple_of(c * rows, rows), rows)
-        return copy(fin.at[i, mine], final_ref.at[i], f_send, f_recv, {"seq": c})
-
-    def call_next():
-        pl.semaphore_signal(go, inc=1, device_id={"seq": z + 1}, device_id_type=MESH)
-
     @pl.when(is_source)
     def _():
-        pl.when(has_prev)(lambda: pl.semaphore_wait(go, 1))
-        for j in range(pieces):
+        for j in range(CHUNKS, pieces):
             give(j).start()
         for j in range(CALL_AFTER):
             sent(j).wait_send()
@@ -221,7 +232,7 @@
     @pl.when(is_master)
     def _():
         for d, r in enumerate(twins):
-            for j in range(pieces):
+            for j in range(CHUNKS, pieces):
                 give_twin(j, d).start()
         pl.when(z > 0)(give_queries)
 
@@ -275,19 +286,34 @@
         kv[mz, x, 1] = nv_v[...]
         get_key.wait()
 
-        def train(c, last):
-            for d in range(m):
-                r = lax.rem(x + d, m)
+        def train(c, split=False, last=False):
+            def await_block(r):
                 pl.when((c != mz) | (r != x))(lambda: take(c, r).wait_recv())
+
+            await_block(x)
+            if not split:
+                for r in twins:
+                    await_block(r)
             scales = [sums(i) for i in range(3)]
             ws = [state[i].astype(BF16) for i in range(3)]
+            if split:
+                for d, r in enumerate([x] + twins):
+                    if d > 0:
+                        await_block(r)
+                    grads = span_grads(kv[c, r, 0], kv[c, r, 1], ws, scales)
+                    if d > 0:
+                        grads = [grad[i] + grads[i] for i in range(3)]
+                    if d < m - 1:
+                        for i in range(3):
+                            grad[i] = grads[i]
             for i in range(3):
                 w = state[i] * scales[i]
                 state[i] = w
                 halves[c, i] = w.astype(BF16)
-            k = kv[c, :, 0].reshape(m * tok, head)
-            nv = kv[c, :, 1].reshape(m * tok, head)
-            grads = span_grads(k, nv, ws, scales)
+            if not split:
+                k = kv[c, :, 0].reshape(m * tok, head)
+                nv = kv[c, :, 1].reshape(m * tok, head)
+                grads = span_grads(k, nv, ws, scales)
             if last:
                 for i in range(3):
                     grad[i] = grads[i]
@@ -298,8 +324,9 @@
             if not last:
                 pl.when(c > 0)(lambda: give_half(c).start())
 
-        pl.loop(0, n - 1)(lambda c: train(c, False))
-        train(n - 1, True)
+        pl.loop(0, 2)(lambda c: train(c, split=True))
+        pl.loop(2, n - 1)(train)
+        train(n - 1, last=True)
 
         far = jnp.where(mz < n // 2, n - 1, 0)
         for i in range(3):

time: 30.3 us -> 30.2 us (level)
  no operation moved by 1% of the time
where the time goes in v5:
time: 30.2 us; the launch traced here: 30 us
  Pallas kernels  28.1 us (93%)
  between operations  1.93 us (6%)
    pallas_call x1, Pallas kernels, per_device(): pl.pallas_call(functools.partial(kernel, n, m, nb), out_shape=(pltpu.VMEM...  27.3 us
    pallas_call x1, Pallas kernels, per_device(): pl.pallas_call(finish, out_shape=(jax.ShapeDtypeStruct((tok, head), BF16)...  0.74 us

profile of v5, /device:TPU:0, one launch (start us, length us, event | category | flops | bytes accessed | tf_op | source)
XLA Modules:
  0.0 30.0 jit_solution(1022779871139153237)
XLA Ops:
  1.9 27.3 %shard_map.86 = (bf16[256,256]{1,0:T(8,128)(2,1)S(1)}, bf16[3,64,256]{2,1,0:T(8,128)(2,1)S(1)}) custom-call(s32[1]{0:T(128)S(6)} %copy.9.start_ref, s32[1,1]{1,0:T(1,128)S(6)} %copy.10.len_ref, bf16[256,256]{1,0:T(8,128)(2,1)} %bitcast.5, bf16[256,256]{1,0:T(8,128)(2,1)} %bitcast.6, f32[1,256]{1,0:T(1,128)} %rate_ref.1, bf16[256,256]{1,0:T(8,128)(2,1)} %bitcast.7, ...), custom_call_target="tpu_custom_call" | custom-call | tf_op jit(solution)/shard_map/pallas_call | solution.py:399
  29.3 0.7 %shard_map.87 = (bf16[256,256]{1,0:T(8,128)(2,1)}, f32[3,64,256]{2,1,0:T(8,128)}) custom-call(bf16[256,256]{1,0:T(8,128)(2,1)S(1)} %get-tuple-element.6.out_ref, bf16[3,64,256]{2,1,0:T(8,128)(2,1)S(1)} %get-tuple-element.7.final_ref), custom_call_target="tpu_custom_call" | custom-call | tf_op jit(solution)/shard_map/pallas_call | solution.py:439

commit v6 on v5

--- a/solution.py
+++ b/solution.py
@@ -66,7 +66,7 @@
 
 def kernel(
     n, m, nb, start_ref, len_ref, key_ref, value_ref, rate_ref, q_ref, init_ref, out_ref, final_ref,
-    kv, queue, outs, halves, state, root, grad, fin, val_v, rate_v, q_v, nv_v,
+    kv, queue, outs, halves, state, root, fin, val_v, rate_v, q_v, nv_v,
     in_sem, kv_send, twin_send, part_recv, kv_recv, pass_send, q_send, q_recv, h_send, h_recv, o_send, o_recv, f_send, f_recv,
     go, qgo,
 ):
@@ -286,47 +286,28 @@
         kv[mz, x, 1] = nv_v[...]
         get_key.wait()
 
-        def train(c, split=False, last=False):
-            def await_block(r):
+        def train(c, last):
+            for d in range(m):
+                r = lax.rem(x + d, m)
                 pl.when((c != mz) | (r != x))(lambda: take(c, r).wait_recv())
-
-            await_block(x)
-            if not split:
-                for r in twins:
-                    await_block(r)
             scales = [sums(i) for i in range(3)]
             ws = [state[i].astype(BF16) for i in range(3)]
-            if split:
-                for d, r in enumerate([x] + twins):
-                    if d > 0:
-                        await_block(r)
-                    grads = span_grads(kv[c, r, 0], kv[c, r, 1], ws, scales)
-                    if d > 0:
-                        grads = [grad[i] + grads[i] for i in range(3)]
-                    if d < m - 1:
-                        for i in range(3):
-                            grad[i] = grads[i]
             for i in range(3):
                 w = state[i] * scales[i]
                 state[i] = w
                 halves[c, i] = w.astype(BF16)
-            if not split:
-                k = kv[c, :, 0].reshape(m * tok, head)
-                nv = kv[c, :, 1].reshape(m * tok, head)
-                grads = span_grads(k, nv, ws, scales)
+            k = kv[c, :, 0].reshape(m * tok, head)
+            nv = kv[c, :, 1].reshape(m * tok, head)
+            grads = span_grads(k, nv, ws, scales)
             if last:
-                for i in range(3):
-                    grad[i] = grads[i]
                 give_half(c).start()
-                grads = [grad[i] for i in range(3)]
             for i, y in enumerate(newton(grads)):
                 state[i] = state[i] + (step_size / half_root) * y
             if not last:
                 pl.when(c > 0)(lambda: give_half(c).start())
 
-        pl.loop(0, 2)(lambda c: train(c, split=True))
-        pl.loop(2, n - 1)(train)
-        train(n - 1, last=True)
+        pl.loop(0, n - 1)(lambda c: train(c, False))
+        train(n - 1, True)
 
         far = jnp.where(mz < n // 2, n - 1, 0)
         for i in range(3):
@@ -411,7 +392,6 @@
             pltpu.VMEM((n,) + init_weights.shape, BF16),
             pltpu.VMEM(init_weights.shape, F32),
             pltpu.VMEM((3, 1, hidden), F32),
-            pltpu.VMEM(init_weights.shape, F32),
             pltpu.VMEM(init_weights.shape, BF16),
             pltpu.VMEM((tok, head), BF16),
             pltpu.VMEM((1, tok), F32),

time: 30.2 us -> 30.2 us (level)
  no operation moved by 1% of the time
where the time goes in v6:
time: 30.2 us; the launch traced here: 30.1 us
  Pallas kernels  28.1 us (93%)
  between operations  1.93 us (6%)
    pallas_call x1, Pallas kernels, per_device(): pl.pallas_call(functools.partial(kernel, n, m, nb), out_shape=(pltpu.VMEM...  27.4 us
    pallas_call x1, Pallas kernels, per_device(): pl.pallas_call(finish, out_shape=(jax.ShapeDtypeStruct((tok, head), BF16)...  0.74 us

profile of v6, /device:TPU:0, one launch (start us, length us, event | category | flops | bytes accessed | tf_op | source)
XLA Modules:
  0.0 30.1 jit_solution(12744957144472971160)
XLA Ops:
  1.9 27.4 %shard_map.86 = (bf16[256,256]{1,0:T(8,128)(2,1)S(1)}, bf16[3,64,256]{2,1,0:T(8,128)(2,1)S(1)}) custom-call(s32[1]{0:T(128)S(6)} %copy.9.start_ref, s32[1,1]{1,0:T(1,128)S(6)} %copy.10.len_ref, bf16[256,256]{1,0:T(8,128)(2,1)} %bitcast.5, bf16[256,256]{1,0:T(8,128)(2,1)} %bitcast.6, f32[1,256]{1,0:T(1,128)} %rate_ref.1, bf16[256,256]{1,0:T(8,128)(2,1)} %bitcast.7, ...), custom_call_target="tpu_custom_call" | custom-call | tf_op jit(solution)/shard_map/pallas_call | solution.py:380
  29.3 0.7 %shard_map.87 = (bf16[256,256]{1,0:T(8,128)(2,1)}, f32[3,64,256]{2,1,0:T(8,128)}) custom-call(bf16[256,256]{1,0:T(8,128)(2,1)S(1)} %get-tuple-element.6.out_ref, bf16[3,64,256]{2,1,0:T(8,128)(2,1)S(1)} %get-tuple-element.7.final_ref), custom_call_target="tpu_custom_call" | custom-call | tf_op jit(solution)/shard_map/pallas_call | solution.py:419

commit v7 on v4

--- a/solution.py
+++ b/solution.py
@@ -8,9 +8,9 @@
 from jax.sharding import PartitionSpec as P
 
 NS_STEPS = 5
-CHUNKS = 2
-CALL_AFTER = 1
-QUERY_AFTER = 2
+CHUNKS = 4
+CALL_AFTER = 2
+QUERY_AFTER = 4
 MESH = pl.DeviceIdType.MESH
 step_size = 0.1
 norm_eps = 1e-07

time: 30.3 us -> 30.2 us (level)
  no operation moved by 1% of the time
where the time goes in v7:
time: 30.2 us; the launch traced here: 30 us
  Pallas kernels  28.1 us (93%)
  between operations  1.93 us (6%)
    pallas_call x1, Pallas kernels, per_device(): pl.pallas_call(functools.partial(kernel, n, m, nb), out_shape=(pltpu.VMEM...  27.3 us
    pallas_call x1, Pallas kernels, per_device(): pl.pallas_call(finish, out_shape=(jax.ShapeDtypeStruct((tok, head), BF16)...  0.74 us

profile of v7, /device:TPU:0, one launch (start us, length us, event | category | flops | bytes accessed | tf_op | source)
XLA Modules:
  0.0 30.0 jit_solution(6816307633422860454)
XLA Ops:
  1.9 27.3 %shard_map.86 = (bf16[256,256]{1,0:T(8,128)(2,1)S(1)}, bf16[3,64,256]{2,1,0:T(8,128)(2,1)S(1)}) custom-call(s32[1]{0:T(128)S(6)} %copy.9.start_ref, s32[1,1]{1,0:T(1,128)S(6)} %copy.10.len_ref, bf16[256,256]{1,0:T(8,128)(2,1)} %bitcast.5, bf16[256,256]{1,0:T(8,128)(2,1)} %bitcast.6, f32[1,256]{1,0:T(1,128)} %rate_ref.1, bf16[256,256]{1,0:T(8,128)(2,1)} %bitcast.7, ...), custom_call_target="tpu_custom_call" | custom-call | tf_op jit(solution)/shard_map/pallas_call | solution.py:372
  29.3 0.7 %shard_map.87 = (bf16[256,256]{1,0:T(8,128)(2,1)}, f32[3,64,256]{2,1,0:T(8,128)}) custom-call(bf16[256,256]{1,0:T(8,128)(2,1)S(1)} %get-tuple-element.6.out_ref, bf16[3,64,256]{2,1,0:T(8,128)(2,1)S(1)} %get-tuple-element.7.final_ref), custom_call_target="tpu_custom_call" | custom-call | tf_op jit(solution)/shard_map/pallas_call | solution.py:412
